TPU v7x, 128 devices: a whole 4x4x4 slice. The times are simulated.
128 devices in a mesh: seq: 16 (over y, x), exp: 8 (over z, core).
Axes of the slice: x: 4, y: 4, z: 4, core: 2. Of those that a mesh axis runs over, the one named last changes fastest.
Arguments:
- queries: bfloat16 [2048, 8192], P('seq', 'exp'), may hold values from -0.5 to 0.5
- keys: bfloat16 [2048, 8192], P('seq', 'exp'), may hold values from -0.5 to 0.5
- values: bfloat16 [2048, 8192], P('seq', 'exp'), may hold values from -6 to 6
- attn_grad: bfloat16 [2048, 8192], P('seq', 'exp'), may hold values from -6 to 6
- log_decay: float32 [2048, 64], P('seq', 'exp'), may hold values from -0.75 to 0, as said below
- moe_grad: bfloat16 [2048, 6144], P('seq', 'exp'), may hold values from -6 to 6
- gate_probs: bfloat16 [2048, 2], P('seq'), may hold values from 0.099609375 to 0.8984375
- expert_ids: int32 [2048, 2], P('seq'), may hold values from 0 to 7, all different within a row; in each aligned block of 128 rows (0 to 127, 128 to 255, ...) at most 48 rows name the same one
- hidden_acts: bfloat16 [8, 768, 9216], P('exp', None, 'seq'), may hold values from -0.3125 to 0.3125
- down_weight: bfloat16 [8, 9216, 6144], P('exp', 'seq'), may hold values from -0.0625 to 0.0625
Outputs:
- query_grad: bfloat16 [2048, 8192], P('seq', 'exp')
- key_grad: bfloat16 [2048, 8192], P('seq', 'exp')
- value_grad: bfloat16 [2048, 8192], P('seq', 'exp')
- hidden_grad: bfloat16 [8, 768, 9216], P('exp', None, 'seq')
- weight_grad: bfloat16 [8, 9216, 6144], P('exp', 'seq')
- gate_grad: float32 [2048, 2], P('seq')
Inputs may be any that keep to these rules, and one draw needn't show every extreme that they name: `expert_ids`: each row names 2 different experts. In the 128 rows of one index of seq no expert is named by more than 48 rows, and every draw has such a block where some expert is named by exactly 48 rows. `log_decay`: log decay of each head at each position; never positive.
All inputs are finite; a program needn't handle non-finite values.
Results may differ from a plain program's by a relative error of at most 0.005.
Values may be sent and summed in bfloat16 or wider, within the bound.
A program may use at most 128 MiB of HBM per device.

v0:
```python
import jax
import jax.numpy as jnp
from jax import lax
from jax.sharding import PartitionSpec as P

precise = lax.Precision.HIGHEST


def prefix(part, axis, combine, identity, reverse):
    count = lax.axis_size(axis)
    place = lax.axis_index(axis)
    ahead = count - 1 - place if reverse else place
    gathered = jax.tree.map(lambda a: lax.all_gather(a, axis), part)
    state = jax.tree.map(lambda a, e: jnp.zeros_like(a) + jnp.asarray(e, a.dtype), part, identity)

    def one(lap, state):
        source = count - 1 - lap if reverse else lap
        return combine(
            state, jax.tree.map(lambda a: lax.dynamic_index_in_dim(a, source, 0, False), gathered)
        )

    return lax.fori_loop(0, ahead, one, state)


def chain_combine(earlier, latter):
    return (jnp.exp(latter[1])[:, None, None] * earlier[0] + latter[0], earlier[1] + latter[1])


def on_device(
    queries,
    keys,
    values,
    attn_grad,
    log_decay,
    moe_grad,
    gate_probs,
    expert_ids,
    hidden_acts,
    down_weight,
):
    tok_count = queries.shape[0]
    head_count = log_decay.shape[1]
    head_width = queries.shape[1] // head_count
    shaped = (tok_count, head_count, head_width)
    query_f = queries.astype(jnp.float32).reshape(shaped)
    key_f = keys.astype(jnp.float32).reshape(shaped)
    value_f = values.astype(jnp.float32).reshape(shaped)
    grad_f = attn_grad.astype(jnp.float32).reshape(shaped)
    cumul = jnp.cumsum(log_decay, axis=0)
    total = cumul[-1]
    tail_w = jnp.exp(total[None, :] - cumul)
    lead_w = jnp.exp(cumul)
    state_kv = jnp.einsum("th,thi,thj->hij", tail_w, key_f, value_f, precision=precise)
    state_qg = jnp.einsum("th,thi,thj->hij", lead_w, query_f, grad_f, precision=precise)
    zero_state = jnp.zeros_like(state_kv)
    zero_gain = jnp.zeros_like(total)
    incoming = prefix((state_kv, total), "seq", chain_combine, (zero_state, zero_gain), False)[0]
    upcoming = prefix((state_qg, total), "seq", chain_combine, (zero_state, zero_gain), True)[0]
    causal = jnp.arange(tok_count)[:, None] >= jnp.arange(tok_count)[None, :]
    spread = cumul.T[:, :, None] - cumul.T[:, None, :]
    decay_mask = jnp.exp(jnp.where(causal[None], spread, -jnp.inf))
    grad_scores = jnp.einsum("thj,shj->hts", grad_f, value_f, precision=precise) * decay_mask
    qk_scores = jnp.einsum("thi,shi->hts", query_f, key_f, precision=precise) * decay_mask
    query_g = jnp.einsum("hts,shi->thi", grad_scores, key_f, precision=precise)
    query_g = query_g + lead_w[:, :, None] * jnp.einsum(
        "thj,hij->thi", grad_f, incoming, precision=precise
    )
    key_g = jnp.einsum("hts,thi->shi", grad_scores, query_f, precision=precise)
    key_g = key_g + tail_w[:, :, None] * jnp.einsum(
        "shj,hij->shi", value_f, upcoming, precision=precise
    )
    value_g = jnp.einsum("hts,thj->shj", qk_scores, grad_f, precision=precise)
    value_g = value_g + tail_w[:, :, None] * jnp.einsum(
        "shi,hij->shj", key_f, upcoming, precision=precise
    )
    flat_width = head_count * head_width
    query_grad = query_g.reshape(tok_count, flat_width).astype(jnp.bfloat16)
    key_grad = key_g.reshape(tok_count, flat_width).astype(jnp.bfloat16)
    value_grad = value_g.reshape(tok_count, flat_width).astype(jnp.bfloat16)
    expert_here = lax.axis_index("exp")
    cap_size = hidden_acts.shape[1] // lax.axis_size("seq")
    chosen_here = expert_ids == expert_here
    routed = jnp.any(chosen_here, axis=1)
    token_gate = jnp.sum(jnp.where(chosen_here, gate_probs.astype(jnp.float32), 0.0), axis=1)
    slot_rank = jnp.cumsum(routed.astype(jnp.int32)) - 1
    slot_ids = jnp.arange(cap_size, dtype=jnp.int32)
    selector = ((slot_rank[None, :] == slot_ids[:, None]) & routed[None, :]).astype(jnp.float32)
    slot_gate = jnp.dot(selector, token_gate, precision=precise).astype(jnp.bfloat16)
    whole_rows = lax.all_gather(moe_grad, "exp", axis=1, tiled=True)
    slot_rows = jnp.dot(
        selector.astype(jnp.bfloat16), whole_rows, preferred_element_type=jnp.float32
    ).astype(jnp.bfloat16)
    weight_here = down_weight[0]
    hidden_here = hidden_acts[0]
    piece_rows = lax.all_gather(slot_rows, "seq", axis=0, tiled=True)
    piece_gate = lax.all_gather(slot_gate, "seq", axis=0, tiled=True)
    back_rows = lax.dot_general(
        piece_rows, weight_here, (((1,), (1,)), ((), ())), preferred_element_type=jnp.float32
    )
    gate_col = piece_gate.astype(jnp.float32)[:, None]
    hidden_out = (gate_col * back_rows).astype(jnp.bfloat16)
    piece_parts = jnp.sum(back_rows * hidden_here.astype(jnp.float32), axis=1)
    slot_parts = piece_parts
    weighted = (gate_col * piece_rows.astype(jnp.float32)).astype(jnp.bfloat16)
    grad_sum = lax.dot_general(
        hidden_here, weighted, (((0,), (0,)), ((), ())), preferred_element_type=jnp.float32
    )
    grad_sum, hidden_out, slot_parts = (grad_sum, hidden_out, slot_parts)
    own_parts = lax.psum_scatter(slot_parts, "seq", scatter_dimension=0, tiled=True)
    per_token = jnp.dot(selector.T, own_parts, precision=precise)
    local_gate = jnp.where(chosen_here, per_token[:, None], 0.0)
    gate_grad = lax.psum(local_gate, "exp")
    return (
        query_grad,
        key_grad,
        value_grad,
        hidden_out[None],
        grad_sum.astype(jnp.bfloat16)[None],
        gate_grad,
    )


def solution(mesh):
    return jax.shard_map(
        on_device,
        mesh=mesh,
        in_specs=(
            P("seq", "exp"),
            P("seq", "exp"),
            P("seq", "exp"),
            P("seq", "exp"),
            P("seq", "exp"),
            P("seq", "exp"),
            P("seq", None),
            P("seq", None),
            P("exp", None, "seq"),
            P("exp", "seq", None),
        ),
        out_specs=(
            P("seq", "exp"),
            P("seq", "exp"),
            P("seq", "exp"),
            P("exp", None, "seq"),
            P("exp", "seq", None),
            P("seq", None),
        ),
        check_vma=False,
    )
```

profile of v0, /device:TPU:1, one launch (start us, length us, event | category | flops | bytes accessed | tf_op | source)
XLA Modules:
  0.0 343.7 jit_solution(9725436786065418335)
XLA Ops:
  10.2 1.2 fusion.21
  13.8 1.5 fusion.18
  16.5 21.5 %all-gather.8.cloned.1.call-done = bf16[128,6144]{1,0:T(8,128)(2,1)} async-done(((bf16[128,768]{1,0:T(8,128)(2,1)}), bf16[128,6144]{1,0:T(8,128)(2,1)}) %all-gather.8.cloned.1.call-update) | async-done | bytes 1572880 | tf_op jit(solution)/shard_map/all_gather | solution.py:89
  37.9 2.6 convolution_convert_fusion
  42.1 33.4 %all-reduce = bf16[768]{0:T(1024)(128)(2,1)S(1)} all-reduce(bf16[768]{0:T(1024)(128)(2,1)S(1)} %dynamic-update-slice), channel_id=1, replica_groups=mesh['seq'=16,'exp'=8] {'seq'}, use_global_device_ids=true, to_apply=%add | all-reduce | flops 768 | bytes 3072
  76.2 15.0 %all-gather.2 = f32[16,1,8]{2,1,0:T(1,128)S(1)} all-gather(f32[1,1,8]{2,1,0:T(1,128)S(1)} %get-tuple-element.211), channel_id=1, replica_groups=mesh['seq'=16,'exp'=8] {'seq'}, dimensions={0}, use_global_device_ids=true | all-gather | bytes 544 | tf_op jit(solution)/shard_map/all_gather | solution.py:13
  91.9 19.4 %all-gather.12.cloned.1.call-done = f32[128,128,128]{2,1,0:T(8,128)} async-done(((f32[8,128,128]{2,1,0:T(8,128)}), f32[128,128,128]{2,1,0:T(8,128)}) %all-gather.12.cloned.1.call-update) | async-done | bytes 8388624 | tf_op jit(solution)/shard_map/all_gather | solution.py:13
  113.2 70.5 %all-gather.14.cloned.1.call-done = f32[128,128,128]{2,1,0:T(8,128)} async-done(((f32[8,128,128]{2,1,0:T(8,128)}), f32[128,128,128]{2,1,0:T(8,128)}) %all-gather.14.cloned.1.call-update) | async-done | bytes 8388624 | tf_op jit(solution)/shard_map/all_gather | solution.py:13
  183.7 18.6 %while.27 = (s32[]{:T(128)}, f32[8,128,128]{2,1,0:T(8,128)S(1)}, s32[]{:T(128)}, f32[16,8]{1,0:T(8,128)S(1)}, f32[16,8,128,128]{3,2,1,0:T(8,128)}, /*index=5*/s32[]{:T(128)}, s32[]{:T(128)}, s32[]{:T(128)}, s32[]{:T(128)}) while((s32[]{:T(128)}, f32[8,128,128]{2,1,0:T(8,128)S(1)}, s32[]{:T(128)}, f32[16,8]{1,0:T(8,128)S(1)}, ...), condition=%wide.region_4.5_spmd, body=%wide.region_3.4_spmd.sunk | while | flops 262150 | bytes 1573115 | solution.py:22
  183.8 1.2 bitcast_add_fusion.5
  185.0 1.2 bitcast_add_fusion.5
  186.2 1.2 bitcast_add_fusion.5
  187.5 1.2 bitcast_add_fusion.5
  188.7 1.2 bitcast_add_fusion.5
  189.9 1.2 bitcast_add_fusion.5
  191.2 1.2 bitcast_add_fusion.5
  194.9 1.2 bitcast_add_fusion.5
  196.1 1.2 bitcast_add_fusion.5
  197.4 1.2 bitcast_add_fusion.5
  206.1 55.5 %all-gather.10.cloned.1.call-done = bf16[768,6144]{1,0:T(8,128)(2,1)} async-done(((bf16[48,6144]{1,0:T(8,128)(2,1)}), bf16[768,6144]{1,0:T(8,128)(2,1)}) %all-gather.10.cloned.1.call-update) | async-done | bytes 9437200 | tf_op jit(solution)/shard_map/all_gather | solution.py:95
  261.6 11.6 %multiply_reduce_fusion = (f32[768]{0:T(1024)S(1)}, bf16[1,768,576]{1,2,0:T(8,128)(2,1)}) fusion(bf16[1,768,576]{1,2,0:T(8,128)(2,1)} %param.22, f32[768]{0:T(1024)S(1)} %convert_element_type.83, bf16[768,6144]{1,0:T(8,128)(2,1)} %all-gather.10.cloned.1.call-done, bf16[1,576,6144]{2,1,0:T(8,128)(2,1)} %param.23), kind=kOutput, calls=%fused_computation.12 | convolution fusion | flops 5438028800 | bytes 18290688 | tf_op jit(solution)/shard_map/dot_general | solution.py:97
  273.2 31.2 %all-reduce.1 = f32[768]{0:T(1024)S(1)} all-reduce(f32[768]{0:T(1024)S(1)} %get-tuple-element.206), channel_id=4, replica_groups=mesh['seq'=16,'exp'=8] {'seq'}, use_global_device_ids=true, to_apply=%region_9.10.clone | all-reduce | flops 768 | bytes 6144
  304.5 20.6 %psum.7 = f32[128,2]{0,1:T(2,128)} all-reduce(f32[128,2]{0,1:T(2,128)S(1)} %broadcast_select_fusion), channel_id=1, replica_groups=mesh['seq'=16,'exp'=8] {'exp'}, use_global_device_ids=true, to_apply=%region_10.11 | all-reduce | flops 256 | bytes 2048 | tf_op jit(solution)/shard_map/psum | solution.py:112
  325.1 12.0 %fusion.3 = bf16[1,576,6144]{2,1,0:T(8,128)(2,1)} fusion(bf16[768,6144]{1,0:T(8,128)(2,1)} %all-gather.10.cloned.1.call-done, f32[768]{0:T(1024)S(1)} %convert_element_type.83, bf16[1,768,576]{1,2,0:T(8,128)(2,1)S(1)} %copy-done.2), kind=kOutput, calls=%fused_computation.8 | convolution fusion | flops 5453512704 | bytes 17402880 | tf_op jit(solution)/shard_map/dot_general | solution.py:105
  (72 shorter events, 20.3 us)
Async XLA Ops:
  7.2 3.0 copy-start
  7.2 33.4 %copy-start.1 = (u32[128]{0:T(128)S(1)}, u32[128]{0:T(128)}, u32[]{:S(2)}) copy-start(u32[128]{0:T(128)} %constant.81) | copy-start | bytes 1540
  7.2 30.7 %all-gather.8.cloned.1.call-start = ((), (), s32[]{:S(2)}) async-start(), calls=%async_computation | async-start | bytes 1769472 | tf_op jit(solution)/shard_map/all_gather | solution.py:89
  7.9 103.3 %all-gather.12.cloned.1.call-start = ((), (), s32[]{:S(2)}) async-start(), calls=%async_computation.2 | async-start | bytes 8912896 | tf_op jit(solution)/shard_map/all_gather | solution.py:13
  11.4 172.3 %all-gather.14.cloned.1.call-start = ((), (), s32[]{:S(2)}) async-start(), calls=%async_computation.3 | async-start | bytes 8912896 | tf_op jit(solution)/shard_map/all_gather | solution.py:13
  15.3 246.3 %all-gather.10.cloned.1.call-start = ((), (), s32[]{:S(2)}) async-start(), calls=%async_computation.1 | async-start | bytes 10027008 | tf_op jit(solution)/shard_map/all_gather | solution.py:95
  206.1 119.0 %copy-start.2 = (bf16[1,768,576]{1,2,0:T(8,128)(2,1)S(1)}, bf16[1,768,576]{1,2,0:T(8,128)(2,1)}, u32[]{:S(2)}) copy-start(bf16[1,768,576]{1,2,0:T(8,128)(2,1)} %param.22) | copy-start | bytes 2654212
Sparse Core Ops, SparseCore 0:
  9.7 28.1 all-gather.7
  40.6 70.5 all-gather.11
  113.4 70.2 all-gather.13
  186.2 75.2 all-gather.9
where the time goes:
time: 345 us; the launch traced here: 344 us
  waiting for transfers between devices  168 us (49%)
  blocking collectives  100 us (29%)
  matrix products  33 us (10%)
  other arithmetic  19.2 us (6%)
  between operations  15.2 us (4%)
  local copies, waits for them, and re-layouts  8.11 us (2%)
    all_gather x2, waiting for transfers between devices, prefix(): gathered = jax.tree.map(lambda a: lax.all_gather(a, axis), part)  89.8 us
    unnamed x2, blocking collectives  64.5 us
    all_gather x1, waiting for transfers between devices, on_device(): piece_rows = lax.all_gather(slot_rows, 'seq', axis=0, tiled=True)  55.5 us
    all_gather x1, waiting for transfers between devices, on_device(): whole_rows = lax.all_gather(moe_grad, 'exp', axis=1, tiled=True)  21.5 us
    psum x1, blocking collectives, on_device(): gate_grad = lax.psum(local_gate, 'exp')  20.6 us
    add x15, other arithmetic, chain_combine(): jnp.exp(latter[1])[:, None, None] * earlier[0] + latter[0]  17.9 us
    all_gather x1, blocking collectives, prefix(): gathered = jax.tree.map(lambda a: lax.all_gather(a, axis), part)  15 us
    dot_general x1, matrix products, on_device(): lax.dot_general(hidden_here, weighted, (((0,), (0,)), ((), ())), preferre...  12 us
  transfers between devices with their start and end apart: 4, of which 4 were waited for; matrix products, arithmetic and copies ran while one was open for 11% of the time, Pallas kernels for 0%

commit v1 on v0

--- a/solution.py
+++ b/solution.py
@@ -4,6 +4,17 @@
 from jax.sharding import PartitionSpec as P
 
 precise = lax.Precision.HIGHEST
+
+
+def loops_measure(array_here, shard_axis, row_dim):
+    slots = jax.lax.axis_size(shard_axis)
+    return jax.lax.all_to_all(
+        jnp.tile(array_here, [slots if at == row_dim else 1 for at in range(array_here.ndim)]),
+        concat_axis=row_dim,
+        split_axis=row_dim,
+        tiled=True,
+        axis_name=shard_axis,
+    )
 
 
 def prefix(part, axis, combine, identity, reverse):
@@ -86,7 +97,7 @@
     slot_ids = jnp.arange(cap_size, dtype=jnp.int32)
     selector = ((slot_rank[None, :] == slot_ids[:, None]) & routed[None, :]).astype(jnp.float32)
     slot_gate = jnp.dot(selector, token_gate, precision=precise).astype(jnp.bfloat16)
-    whole_rows = lax.all_gather(moe_grad, "exp", axis=1, tiled=True)
+    whole_rows = loops_measure(moe_grad, "exp", 1)
     slot_rows = jnp.dot(
         selector.astype(jnp.bfloat16), whole_rows, preferred_element_type=jnp.float32
     ).astype(jnp.bfloat16)

time: 345 us -> 319 us (0.925)
  waiting for transfers between devices: 168 us -> 133 us
  starting transfers between devices: 0.16 us -> 6.9 us
  local copies, waits for them, and re-layouts: 8.11 us -> 11.9 us
    all_gather x2, waiting for transfers between devices: 89.8 us -> 56.8 us  [prefix(): gathered = jax.tree.map(lambda a: lax.all_gather(a, axis), part)]
    all_gather x1 -> x0, waiting for transfers between devices: 21.5 us -> none  [on_device(): whole_rows = lax.all_gather(moe_grad, 'exp', axis=1, tiled=True)]
    all_to_all x0 -> x1, waiting for transfers between devices: none -> 20.3 us  [loops_measure(): jax.lax.all_to_all(jnp.tile(array_here, [slots if at == row_dim else 1 fo...]
    all_to_all x0 -> x1, starting transfers between devices: none -> 6.81 us  [loops_measure(): jax.lax.all_to_all(jnp.tile(array_here, [slots if at == row_dim else 1 fo...]
  transfers between devices with their start and end apart: 4 -> 4, of which waited for: 4 -> 3; matrix products, arithmetic and copies ran while one was open for 11% -> 11% of each run, Pallas kernels for 0% -> 0%
where the time goes in v1:
time: 319 us; the launch traced here: 317 us
  waiting for transfers between devices  133 us (42%)
  blocking collectives  98.9 us (31%)
  matrix products  32.8 us (10%)
  other arithmetic  18.5 us (6%)
  between operations  15.3 us (5%)
  local copies, waits for them, and re-layouts  11.9 us (4%)
  starting transfers between devices  6.9 us (2%)
    unnamed x2, blocking collectives  65.4 us
    all_gather x2, waiting for transfers between devices, prefix(): gathered = jax.tree.map(lambda a: lax.all_gather(a, axis), part)  56.8 us
    all_gather x1, waiting for transfers between devices, on_device(): piece_rows = lax.all_gather(slot_rows, 'seq', axis=0, tiled=True)  55.6 us
    psum x1, blocking collectives, on_device(): gate_grad = lax.psum(local_gate, 'exp')  20.6 us
    all_to_all x1, waiting for transfers between devices, loops_measure(): jax.lax.all_to_all(jnp.tile(array_here, [slots if at == row_dim else 1 fo...  20.3 us
    add x15, other arithmetic, chain_combine(): jnp.exp(latter[1])[:, None, None] * earlier[0] + latter[0]  18 us
    all_gather x1, blocking collectives, prefix(): gathered = jax.tree.map(lambda a: lax.all_gather(a, axis), part)  13 us
    dot_general x1, matrix products, on_device(): lax.dot_general(piece_rows, weight_here, (((1,), (1,)), ((), ())), prefer...  11.6 us
  transfers between devices with their start and end apart: 4, of which 3 were waited for; matrix products, arithmetic and copies ran while one was open for 11% of the time, Pallas kernels for 0%

profile of v1, /device:TPU:1, one launch (start us, length us, event | category | flops | bytes accessed | tf_op | source)
XLA Modules:
  0.0 317.5 jit_solution(7576437686698565336)
XLA Ops:
  9.5 1.2 fusion.21
  13.1 1.4 fusion.18
  14.6 2.2 tile.2
  16.7 6.8 %all-to-all-start = ((bf16[128,8,768]{2,0,1:T(8,128)(2,1)}), bf16[128,8,768]{2,0,1:T(8,128)(2,1)S(1)}, u32[]{:S(2)}, u32[]{:S(2)}) async-start(bf16[128,8,768]{2,0,1:T(8,128)(2,1)} %tile.2), calls=%async_computation | async-start | bytes 3145728 | tf_op jit(solution)/shard_map/all_to_all | solution.py:11
  24.0 20.3 %all-to-all-done = bf16[128,8,768]{2,0,1:T(8,128)(2,1)S(1)} async-done(((bf16[128,8,768]{2,0,1:T(8,128)(2,1)}), bf16[128,8,768]{2,0,1:T(8,128)(2,1)S(1)}, u32[]{:S(2)}, u32[]{:S(2)}) %all-to-all-start) | async-done | bytes 1572896 | tf_op jit(solution)/shard_map/all_to_all | solution.py:11
  44.3 1.6 copy.109
  45.8 2.9 convolution_convert_fusion
  50.4 34.2 %all-reduce = bf16[768]{0:T(1024)(128)(2,1)S(1)} all-reduce(bf16[768]{0:T(1024)(128)(2,1)S(1)} %dynamic-update-slice), channel_id=1, replica_groups=mesh['seq'=16,'exp'=8] {'seq'}, use_global_device_ids=true, to_apply=%add | all-reduce | flops 768 | bytes 3072
  85.3 13.0 %all-gather.2 = f32[16,1,8]{2,1,0:T(1,128)S(1)} all-gather(f32[1,1,8]{2,1,0:T(1,128)S(1)} %get-tuple-element.227), channel_id=1, replica_groups=mesh['seq'=16,'exp'=8] {'seq'}, dimensions={0}, use_global_device_ids=true | all-gather | bytes 544 | tf_op jit(solution)/shard_map/all_gather | solution.py:24
  101.0 56.8 %all-gather.11.cloned.1.call-done = f32[128,128,128]{2,1,0:T(8,128)} async-done(((f32[8,128,128]{2,1,0:T(8,128)}), f32[128,128,128]{2,1,0:T(8,128)}) %all-gather.11.cloned.1.call-update) | async-done | bytes 8388624 | tf_op jit(solution)/shard_map/all_gather | solution.py:24
  157.8 18.6 %while.27 = (s32[]{:T(128)}, f32[8,128,128]{2,1,0:T(8,128)S(1)}, s32[]{:T(128)}, f32[16,8]{1,0:T(8,128)S(1)}, f32[16,8,128,128]{3,2,1,0:T(8,128)}, /*index=5*/s32[]{:T(128)}, s32[]{:T(128)}, s32[]{:T(128)}, s32[]{:T(128)}) while((s32[]{:T(128)}, f32[8,128,128]{2,1,0:T(8,128)S(1)}, s32[]{:T(128)}, f32[16,8]{1,0:T(8,128)S(1)}, ...), condition=%wide.region_4.5_spmd, body=%wide.region_3.4_spmd.sunk | while | flops 262150 | bytes 1573115 | solution.py:33
  157.9 1.2 bitcast_add_fusion.5
  159.1 1.2 bitcast_add_fusion.5
  160.3 1.2 bitcast_add_fusion.5
  161.6 1.2 bitcast_add_fusion.5
  169.0 1.2 bitcast_add_fusion.5
  170.2 1.2 bitcast_add_fusion.5
  171.5 1.2 bitcast_add_fusion.5
  175.2 1.2 bitcast_add_fusion.5
  180.2 55.6 %all-gather.7.cloned.1.call-done = bf16[768,6144]{1,0:T(8,128)(2,1)} async-done(((bf16[48,6144]{1,0:T(8,128)(2,1)}), bf16[768,6144]{1,0:T(8,128)(2,1)}) %all-gather.7.cloned.1.call-update) | async-done | bytes 9437200 | tf_op jit(solution)/shard_map/all_gather | solution.py:106
  235.8 11.6 %multiply_reduce_fusion = (f32[768]{0:T(1024)S(1)}, bf16[1,768,576]{1,2,0:T(8,128)(2,1)}) fusion(bf16[1,768,576]{1,2,0:T(8,128)(2,1)} %param.22, f32[768]{0:T(1024)S(1)} %convert_element_type.83, bf16[768,6144]{1,0:T(8,128)(2,1)} %all-gather.7.cloned.1.call-done, bf16[1,576,6144]{2,1,0:T(8,128)(2,1)} %param.23), kind=kOutput, calls=%fused_computation.12 | convolution fusion | flops 5438028800 | bytes 18290688 | tf_op jit(solution)/shard_map/dot_general | solution.py:108
  247.4 31.2 %all-reduce.1 = f32[768]{0:T(1024)S(1)} all-reduce(f32[768]{0:T(1024)S(1)} %get-tuple-element.222), channel_id=4, replica_groups=mesh['seq'=16,'exp'=8] {'seq'}, use_global_device_ids=true, to_apply=%region_9.10.clone | all-reduce | flops 768 | bytes 6144
  278.8 20.6 %psum.7 = f32[128,2]{0,1:T(2,128)} all-reduce(f32[128,2]{0,1:T(2,128)S(1)} %broadcast_select_fusion), channel_id=1, replica_groups=mesh['seq'=16,'exp'=8] {'exp'}, use_global_device_ids=true, to_apply=%region_10.11 | all-reduce | flops 256 | bytes 2048 | tf_op jit(solution)/shard_map/psum | solution.py:123
  299.4 11.6 %fusion.3 = bf16[1,576,6144]{2,1,0:T(8,128)(2,1)} fusion(bf16[768,6144]{1,0:T(8,128)(2,1)} %all-gather.7.cloned.1.call-done, f32[768]{0:T(1024)S(1)} %convert_element_type.83, bf16[1,768,576]{1,2,0:T(8,128)(2,1)S(1)} %copy-done.4), kind=kOutput, calls=%fused_computation.8 | convolution fusion | flops 5453512704 | bytes 17402880 | tf_op jit(solution)/shard_map/dot_general | solution.py:116
  (77 shorter events, 21.3 us)
Async XLA Ops:
  7.2 2.3 copy-start
  7.2 16.4 %copy-start.3 = (bf16[128,2]{0,1:T(2,128)(2,1)S(1)}, bf16[128,2]{0,1:T(2,128)(2,1)}, u32[]{:S(2)}) copy-start(bf16[128,2]{0,1:T(2,128)(2,1)} %param.20) | copy-start | bytes 1540
  7.2 16.4 %copy-start.2 = (s32[128,2]{0,1:T(2,128)S(1)}, s32[128,2]{0,1:T(2,128)}, u32[]{:S(2)}) copy-start(s32[128,2]{0,1:T(2,128)} %param.21) | copy-start | bytes 3076
  7.2 91.8 %all-gather.9.cloned.1.call-start = ((), (), s32[]{:S(2)}) async-start(), calls=%async_computation.2 | async-start | bytes 8912896 | tf_op jit(solution)/shard_map/all_gather | solution.py:24
  10.7 38.1 %copy-start.1 = (u32[128]{0:T(128)S(1)}, u32[128]{0:T(128)}, u32[]{:S(2)}) copy-start(u32[128]{0:T(128)} %constant.81) | copy-start | bytes 1540
  10.7 147.1 %all-gather.11.cloned.1.call-start = ((), (), s32[]{:S(2)}) async-start(), calls=%async_computation.3 | async-start | bytes 8912896 | tf_op jit(solution)/shard_map/all_gather | solution.py:24
  16.7 27.5 %all-to-all-start = ((bf16[128,8,768]{2,0,1:T(8,128)(2,1)}), bf16[128,8,768]{2,0,1:T(8,128)(2,1)S(1)}, u32[]{:S(2)}, u32[]{:S(2)}) async-start(bf16[128,8,768]{2,0,1:T(8,128)(2,1)} %tile.2), calls=%async_computation | async-start | bytes 3145728 | tf_op jit(solution)/shard_map/all_to_all | solution.py:11
  23.6 212.3 %all-gather.7.cloned.1.call-start = ((), (), s32[]{:S(2)}) async-start(), calls=%async_computation.1 | async-start | bytes 10027008 | tf_op jit(solution)/shard_map/all_gather | solution.py:106
  180.2 119.2 %copy-start.4 = (bf16[1,768,576]{1,2,0:T(8,128)(2,1)S(1)}, bf16[1,768,576]{1,2,0:T(8,128)(2,1)}, u32[]{:S(2)}) copy-start(bf16[1,768,576]{1,2,0:T(8,128)(2,1)} %param.22) | copy-start | bytes 2654212
Sparse Core Ops, SparseCore 0:
  10.8 74.4 all-gather.8
  87.4 70.2 all-gather.10
  160.5 75.2 all-gather.6
